TPU v7x, 256 devices: a whole 4x4x8 slice. The times are simulated.
256 devices in a mesh: dp: 4 (over y), sx: 4 (over x_lo, core), sy: 16 (over z, x_hi).
Axes of the slice: x: 4 (x_hi: 2, x_lo: 2; x = x_hi * 2 + x_lo), y: 4, z: 8, core: 2. Of those that a mesh axis runs over, the one named last changes fastest.
Arguments:
- features: bfloat16 [4, 4, 16, 3072, 128], P('dp', 'sx', 'sy'), may hold values from -6 to 6
- cotangent: bfloat16 [4, 4, 16, 3072, 128], P('dp', 'sx', 'sy'), may hold values from -6 to 6
- weights: bfloat16 [27, 128, 128], replicated, may hold values from -0.109375 to 0.109375
- tables: int32 [4, 4, 16, 27, 24], P('dp', 'sx', 'sy'), may hold values from 0 to 56, as said below
- send_lists: int32 [4, 4, 16, 4], P('dp', 'sx', 'sy'), may hold values from 0 to 23, as said below
- counts: int32 [4, 4, 16], P('dp', 'sx', 'sy'), may hold values from 6 to 24, as said below
Outputs:
- output: bfloat16 [4, 4, 16, 3072, 128], P('dp', 'sx', 'sy')
- input_grad: bfloat16 [4, 4, 16, 3072, 128], P('dp', 'sx', 'sy')
- weight_grad: float32 [27, 128, 128], replicated
Inputs may be any that keep to these rules, and one draw needn't show every extreme that they name: `tables`: entries below 24 name a block of the tile, 24 + n * 4 + s' the s'-th sent block of neighbour direction n, 56 the empty block; under offset 27 // 2 every block reads itself. `send_lists`: the 4 blocks of one tile are distinct. `counts`: some tile has all 24 blocks active.
All inputs are finite; a program needn't handle non-finite values.
Results may differ from a plain program's by a relative error of at most 0.001.
Values may be sent and summed in bfloat16 or wider, within the bound.
A program may use at most 64 MiB of HBM per device.

v0:
```python
import math
import jax
import jax.numpy as jnp
from jax import lax
from jax.sharding import PartitionSpec as P

directions = ((-1, -1), (-1, 0), (-1, 1), (0, -1), (0, 1), (1, -1), (1, 0), (1, 1))


def shifted(block, axis, distance):
    devices = range(lax.axis_size(axis))
    route = [(i - distance, i) for i in devices if i - distance in devices]
    return lax.ppermute(block, axis, route)


def padded(cells, sides, width):
    for axis, dim in sides:
        count = lax.axis_size(axis)
        ends = count - 1
        head = lax.slice_in_dim(cells, 0, width, axis=dim)
        tail = lax.slice_in_dim(cells, cells.shape[dim] - width, cells.shape[dim], axis=dim)
        cells = jnp.concatenate(
            [
                lax.ppermute(tail, axis, [(i, (i + 1) % count) for i in range(ends)]),
                cells,
                lax.ppermute(head, axis, [((i + 1) % count, i) for i in range(ends)]),
            ],
            axis=dim,
        )
    return cells


def local(features, cotangent, weights, tables, send_lists, counts):
    num_blocks = tables.shape[4]
    num_sent = send_lists.shape[3]
    offsets = weights.shape[0]
    channels = weights.shape[1]
    width_block = features.shape[3] // num_blocks
    group_size = 4
    active = (jnp.arange(num_blocks) < counts.reshape(())).astype(jnp.bfloat16)[:, None, None]
    active_full = active.astype(jnp.float32)
    blocks_in = features.reshape(num_blocks, width_block, channels) * active
    blocks_grad = cotangent.reshape(num_blocks, width_block, channels) * active
    offset_table = tables.reshape(offsets, num_blocks)
    sent_ids = send_lists.reshape(num_sent)
    groups = jnp.arange(num_blocks // group_size)

    def grad_group(accum, group):
        start = group * group_size
        picks = lax.dynamic_slice_in_dim(offset_table, start, group_size, 1)
        grad_rows = lax.dynamic_slice_in_dim(blocks_grad, start, group_size, 0)
        contrib = jnp.einsum(
            "gvd,kcd->kgvc", grad_rows, weights, preferred_element_type=jnp.float32
        )
        accum = accum.at[picks.reshape(-1)].add(
            contrib.reshape(offsets * group_size, width_block, channels)
        )
        return (accum, None)

    num_ext = num_blocks + 8 * num_sent + 1
    grad_ext, unused_rows = lax.scan(
        grad_group, jnp.zeros((num_ext, width_block, channels), jnp.float32), groups
    )
    halo_grads = grad_ext[num_blocks : num_blocks + 8 * num_sent].reshape(
        8, num_sent * width_block, channels
    )
    received = jnp.zeros((num_sent * width_block, channels), jnp.float32)
    for slot_index, (step_x, step_y) in enumerate(directions):
        portion = halo_grads[slot_index]
        if step_x != 0:
            portion = shifted(portion, "sx", step_x)
        if step_y != 0:
            portion = shifted(portion, "sy", step_y)
        received = received + portion
    local_grad = (
        grad_ext[:num_blocks].at[sent_ids].add(received.reshape(num_sent, width_block, channels))
    )
    input_grad = (local_grad * active_full).astype(jnp.bfloat16).reshape(features.shape)
    outgoing = blocks_in[sent_ids].reshape(1, 1, num_sent * width_block, channels)
    bordered = padded(outgoing, (("sx", 0), ("sy", 1)), 1)
    neighbours = [
        bordered[1 + step_x, 1 + step_y].reshape(num_sent, width_block, channels)
        for step_x, step_y in directions
    ]
    extended = jnp.concatenate(
        [blocks_in] + neighbours + [jnp.zeros((1, width_block, channels), jnp.bfloat16)], axis=0
    )

    def forward_group(accum, group):
        start = group * group_size
        picks = lax.dynamic_slice_in_dim(offset_table, start, group_size, 1)
        gathered = extended[picks]
        grad_rows = lax.dynamic_slice_in_dim(blocks_grad, start, group_size, 0)
        rows_active = lax.dynamic_slice_in_dim(active_full, start, group_size, 0)
        outputs = jnp.einsum("kgvc,kcd->gvd", gathered, weights, preferred_element_type=jnp.float32)
        accum = accum + jnp.einsum(
            "kgvc,gvd->kcd", gathered, grad_rows, preferred_element_type=jnp.float32
        )
        return (accum, (outputs * rows_active).astype(jnp.bfloat16))

    weight_part, outputs = lax.scan(
        forward_group, jnp.zeros((offsets, channels, channels), jnp.float32), groups
    )
    output = outputs.reshape(features.shape)
    total = (
        num_blocks * width_block * lax.axis_size("dp") * lax.axis_size("sx") * lax.axis_size("sy")
    )
    scaled_part = weight_part * (1.0 / math.sqrt(total))
    weight_grad = lax.psum(scaled_part, ("dp", "sx", "sy"))
    return (output, input_grad, weight_grad)


def solution(mesh):
    return jax.shard_map(
        local,
        mesh=mesh,
        in_specs=(
            P("dp", "sx", "sy", None, None),
            P("dp", "sx", "sy", None, None),
            P(),
            P("dp", "sx", "sy", None, None),
            P("dp", "sx", "sy", None),
            P("dp", "sx", "sy"),
        ),
        out_specs=(P("dp", "sx", "sy", None, None), P("dp", "sx", "sy", None, None), P()),
        check_vma=False,
    )
```

profile of v0, /device:TPU:2, one launch (start us, length us, event | category | flops | bytes accessed | tf_op | source)
XLA Modules:
  0.0 617.5 jit_solution(9292657915912878841)
XLA Ops:
  8.5 3.2 constant_dynamic-update-slice_fusion.9
  19.8 184.4 %while.23 = (s32[]{:T(128)}, f32[57,128,128]{2,1,0:T(8,128)}, s32[6]{0:T(128)S(1)}, s32[27,24]{1,0:T(8,128)}, bf16[24,128,128]{2,1,0:T(8,128)(2,1)}, /*index=5*/...) while((s32[]{:T(128)}, f32[57,128,128]{2,1,0:T(8,128)}, s32[6]{0:T(128)S(1)}, ...), condition=%wide.region_4.5_spmd, body=%wide.region_2.0_spmd.sunk | while | flops 454754624 | bytes 43486336 | solution.py:61
  24.3 3.3 copy.22
  27.6 22.9 %scatter_fusion = f32[57,128,128]{2,1,0:T(8,128)} fusion(f32[57,128,128]{2,1,0:T(8,128)} %get-tuple-element.307, s32[108]{0:T(128)S(1)} %fusion.33, f32[108,128,128]{2,1,0:T(8,128)} %bitcast.107), kind=kCustom, calls=%fused_computation.2.clone.1 | custom fusion | flops 1769472 | bytes 21234096 | tf_op jit(solution)/shard_map/while/body/eval_jaxpr/scatter-add | solution.py:55
  55.0 3.3 copy.22
  58.3 22.9 %scatter_fusion = f32[57,128,128]{2,1,0:T(8,128)} fusion(f32[57,128,128]{2,1,0:T(8,128)} %get-tuple-element.307, s32[108]{0:T(128)S(1)} %fusion.33, f32[108,128,128]{2,1,0:T(8,128)} %bitcast.107), kind=kCustom, calls=%fused_computation.2.clone.1 | custom fusion | flops 1769472 | bytes 21234096 | tf_op jit(solution)/shard_map/while/body/eval_jaxpr/scatter-add | solution.py:55
  85.7 3.3 copy.22
  89.1 22.8 %scatter_fusion = f32[57,128,128]{2,1,0:T(8,128)} fusion(f32[57,128,128]{2,1,0:T(8,128)} %get-tuple-element.307, s32[108]{0:T(128)S(1)} %fusion.33, f32[108,128,128]{2,1,0:T(8,128)} %bitcast.107), kind=kCustom, calls=%fused_computation.2.clone.1 | custom fusion | flops 1769472 | bytes 21234096 | tf_op jit(solution)/shard_map/while/body/eval_jaxpr/scatter-add | solution.py:55
  116.4 3.3 copy.22
  119.7 23.0 %scatter_fusion = f32[57,128,128]{2,1,0:T(8,128)} fusion(f32[57,128,128]{2,1,0:T(8,128)} %get-tuple-element.307, s32[108]{0:T(128)S(1)} %fusion.33, f32[108,128,128]{2,1,0:T(8,128)} %bitcast.107), kind=kCustom, calls=%fused_computation.2.clone.1 | custom fusion | flops 1769472 | bytes 21234096 | tf_op jit(solution)/shard_map/while/body/eval_jaxpr/scatter-add | solution.py:55
  147.2 3.3 copy.22
  150.6 22.9 %scatter_fusion = f32[57,128,128]{2,1,0:T(8,128)} fusion(f32[57,128,128]{2,1,0:T(8,128)} %get-tuple-element.307, s32[108]{0:T(128)S(1)} %fusion.33, f32[108,128,128]{2,1,0:T(8,128)} %bitcast.107), kind=kCustom, calls=%fused_computation.2.clone.1 | custom fusion | flops 1769472 | bytes 21234096 | tf_op jit(solution)/shard_map/while/body/eval_jaxpr/scatter-add | solution.py:55
  177.9 3.3 copy.22
  181.3 22.9 %scatter_fusion = f32[57,128,128]{2,1,0:T(8,128)} fusion(f32[57,128,128]{2,1,0:T(8,128)} %get-tuple-element.307, s32[108]{0:T(128)S(1)} %fusion.33, f32[108,128,128]{2,1,0:T(8,128)} %bitcast.107), kind=kCustom, calls=%fused_computation.2.clone.1 | custom fusion | flops 1769472 | bytes 21234096 | tf_op jit(solution)/shard_map/while/body/eval_jaxpr/scatter-add | solution.py:55
  204.3 4.3 collective-permute-start.2
  213.4 3.6 collective-permute-start.6
  223.6 10.0 %collective-permute-done.3 = bf16[3,1,512,128]{3,2,1,0:T(8,128)(2,1)S(1)} collective-permute-done((bf16[3,1,512,128]{3,2,1,0:T(8,128)(2,1)S(1)}, bf16[3,1,512,128]{3,2,1,0:T(8,128)(2,1)S(1)}, u32[]{:S(2)}, u32[]{:S(2)}) %collective-permute-start.3) | collective-permute-done | bytes 393248 | tf_op jit(solution)/shard_map/ppermute | solution.py:26
  233.5 6.1 collective-permute-start.10
  244.8 79.9 %while.24 = (s32[]{:T(128)}, f32[27,128,128]{2,1,0:T(8,128)}, bf16[6,4,128,128]{3,2,1,0:T(8,128)(2,1)}, s32[6]{0:T(128)}, s32[27,24]{1,0:T(8,128)}, /*index=5*/b...) while((s32[]{:T(128)}, f32[27,128,128]{2,1,0:T(8,128)}, ...), condition=%wide.region_1.0_spmd.clone, body=%wide.region_0.1_spmd.clone.sunk | while | flops 906986816 | bytes 33004880 | solution.py:101
  251.0 3.0 fusion.39
  264.3 3.0 fusion.39
  277.6 3.0 fusion.39
  290.9 3.0 fusion.39
  304.2 3.0 fusion.39
  317.5 3.0 fusion.39
  324.7 4.2 collective-permute-start.7
  328.9 4.3 collective-permute-start.4
  337.5 6.1 collective-permute-start.15
  344.9 6.1 collective-permute-start.8
  353.8 9.3 %collective-permute-done.15 = f32[512,128]{1,0:T(8,128)S(1)} collective-permute-done((f32[512,128]{1,0:T(8,128)}, f32[512,128]{1,0:T(8,128)S(1)}, u32[]{:S(2)}, u32[]{:S(2)}) %collective-permute-start.15) | collective-permute-done | bytes 262176 | tf_op jit(solution)/shard_map/ppermute | solution.py:13
  363.1 5.7 collective-permute-done.8
  371.9 235.9 %all-reduce.2.cloned.1.call-done = f32[27,128,128]{2,1,0:T(8,128)} async-done(((f32[27,128,128]{2,1,0:T(8,128)}), f32[27,128,128]{2,1,0:T(8,128)}) %all-reduce.2.cloned.1.call-update) | async-done | bytes 1769488 | tf_op jit(solution)/shard_map/psum | solution.py:109
  (154 shorter events, 120.0 us)
Async XLA Ops:
  7.2 600.6 %all-reduce.2.cloned.1.call-start = ((), (), s32[]{:S(2)}) async-start(), calls=%async_computation | async-start | bytes 3538944 | tf_op jit(solution)/shard_map/psum | solution.py:109
  8.5 8.2 %copy-start.3 = (s32[1,1,1,27,24]{3,4,2,1,0:T(8,128)S(1)}, s32[1,1,1,27,24]{3,4,2,1,0:T(8,128)}, u32[]{:S(2)}) copy-start(s32[1,1,1,27,24]{3,4,2,1,0:T(8,128)} %param.13) | copy-start | bytes 7780
  12.3 191.9 %collective-permute-start.1 = (bf16[1,1,512,128]{3,2,1,0:T(8,128)(2,1)S(1)}, bf16[1,1,512,128]{3,2,1,0:T(8,128)(2,1)S(1)}, u32[]{:S(2)}, u32[]{:S(2)}) collective-permute-start(bf16[1,1,512,128]{3,2,1,0:T(8,128)(2,1)S(1)} %bitcast.116), channel_id=1, source_target_pairs={{16,0},{32,16},{48,32},{17,1},{33,17},{49,33},{18,2},{34,18},{50,3... | collective-permute-start | bytes 393224 | tf_op jit(solution)/shard_map/ppermute | solution.py:26
  14.3 189.9 %collective-permute-start = (bf16[1,1,512,128]{3,2,1,0:T(8,128)(2,1)S(1)}, bf16[1,1,512,128]{3,2,1,0:T(8,128)(2,1)S(1)}, u32[]{:S(2)}, u32[]{:S(2)}) collective-permute-start(bf16[1,1,512,128]{3,2,1,0:T(8,128)(2,1)S(1)} %bitcast.117), channel_id=1, source_target_pairs={{0,16},{16,32},{32,48},{1,17},{17,33},{33,49},{2,18},{18,34},{34,5... | collective-permute-start | bytes 393224 | tf_op jit(solution)/shard_map/ppermute | solution.py:24
  204.3 16.7 %collective-permute-start.2 = (bf16[3,1,512,128]{3,2,1,0:T(8,128)(2,1)S(1)}, bf16[3,1,512,128]{3,2,1,0:T(8,128)(2,1)S(1)}, u32[]{:S(2)}, u32[]{:S(2)}) collective-permute-start(bf16[3,1,512,128]{3,2,1,0:T(8,128)(2,1)S(1)} %pad_maximum_fusion), channel_id=1, source_target_pairs={{0,1},{1,2},{2,3},{3,4},{4,5},{5,6},{6,7},{7,8},{8,9},{9,10},{10,1... | collective-permute-start | bytes 1179656 | tf_op jit(solution)/shard_map/ppermute | solution.py:24
  211.4 113.2 %collective-permute-start.14 = (f32[512,128]{1,0:T(8,128)}, f32[512,128]{1,0:T(8,128)}, u32[]{:S(2)}, u32[]{:S(2)}) collective-permute-start(f32[512,128]{1,0:T(8,128)} %bitcast.30), channel_id=1, source_target_pairs={{0,16},{16,32},{32,48},{1,17},{17,33},{33,49},{2,18},{18,34},{34,5... | collective-permute-start | bytes 786440 | tf_op jit(solution)/shard_map/ppermute | solution.py:13
  213.4 115.5 %collective-permute-start.6 = (f32[512,128]{1,0:T(8,128)}, f32[512,128]{1,0:T(8,128)}, u32[]{:S(2)}, u32[]{:S(2)}) collective-permute-start(f32[512,128]{1,0:T(8,128)} %bitcast.24), channel_id=1, source_target_pairs={{16,0},{32,16},{48,32},{17,1},{33,17},{49,33},{18,2},{34,18},{50,3... | collective-permute-start | bytes 786440 | tf_op jit(solution)/shard_map/ppermute | solution.py:13
  217.0 119.1 %collective-permute-start.13 = (f32[512,128]{1,0:T(8,128)}, f32[512,128]{1,0:T(8,128)}, u32[]{:S(2)}, u32[]{:S(2)}) collective-permute-start(f32[512,128]{1,0:T(8,128)} %bitcast.29), channel_id=1, source_target_pairs={{0,16},{16,32},{32,48},{1,17},{17,33},{33,49},{2,18},{18,34},{34,5... | collective-permute-start | bytes 786440 | tf_op jit(solution)/shard_map/ppermute | solution.py:13
  218.9 118.5 %collective-permute-start.11 = (f32[512,128]{1,0:T(8,128)}, f32[512,128]{1,0:T(8,128)}, u32[]{:S(2)}, u32[]{:S(2)}) collective-permute-start(f32[512,128]{1,0:T(8,128)} %bitcast.28), channel_id=1, source_target_pairs={{0,16},{16,32},{32,48},{1,17},{17,33},{33,49},{2,18},{18,34},{34,5... | collective-permute-start | bytes 786440 | tf_op jit(solution)/shard_map/ppermute | solution.py:13
  220.9 12.6 %collective-permute-start.3 = (bf16[3,1,512,128]{3,2,1,0:T(8,128)(2,1)S(1)}, bf16[3,1,512,128]{3,2,1,0:T(8,128)(2,1)S(1)}, u32[]{:S(2)}, u32[]{:S(2)}) collective-permute-start(bf16[3,1,512,128]{3,2,1,0:T(8,128)(2,1)S(1)} %pad_maximum_fusion), channel_id=1, source_target_pairs={{1,0},{2,1},{3,2},{4,3},{5,4},{6,5},{7,6},{8,7},{9,8},{10,9},{11,1... | collective-permute-start | bytes 1179656 | tf_op jit(solution)/shard_map/ppermute | solution.py:26
  233.5 110.0 %collective-permute-start.10 = (f32[512,128]{1,0:T(8,128)}, f32[512,128]{1,0:T(8,128)}, u32[]{:S(2)}, u32[]{:S(2)}) collective-permute-start(f32[512,128]{1,0:T(8,128)} %bitcast.27), channel_id=1, source_target_pairs={{0,1},{1,2},{2,3},{3,4},{4,5},{5,6},{6,7},{7,8},{8,9},{9,10},{10,1... | collective-permute-start | bytes 786440 | tf_op jit(solution)/shard_map/ppermute | solution.py:13
  250.9 3.1 copy-start
  256.9 1.2 copy-start.1
  264.3 3.1 copy-start
  270.2 1.2 copy-start.1
  277.6 3.1 copy-start
  283.5 1.2 copy-start.1
  290.9 3.1 copy-start
  296.8 1.2 copy-start.1
  304.2 3.1 copy-start
  310.2 1.2 copy-start.1
  317.5 3.1 copy-start
  323.5 1.2 copy-start.1
  324.7 20.2 %collective-permute-start.7 = (f32[512,128]{1,0:T(8,128)}, f32[512,128]{1,0:T(8,128)S(1)}, u32[]{:S(2)}, u32[]{:S(2)}) collective-permute-start(f32[512,128]{1,0:T(8,128)} %bitcast.127), channel_id=1, source_target_pairs={{16,0},{32,16},{48,32},{17,1},{33,17},{49,33},{18,2},{34,18},{50,3... | collective-permute-start | bytes 786440 | tf_op jit(solution)/shard_map/ppermute | solution.py:13
  328.9 22.1 %collective-permute-start.4 = (f32[512,128]{1,0:T(8,128)}, f32[512,128]{1,0:T(8,128)S(1)}, u32[]{:S(2)}, u32[]{:S(2)}) collective-permute-start(f32[512,128]{1,0:T(8,128)} %bitcast.126), channel_id=1, source_target_pairs={{16,0},{32,16},{48,32},{17,1},{33,17},{49,33},{18,2},{34,18},{50,3... | collective-permute-start | bytes 786440 | tf_op jit(solution)/shard_map/ppermute | solution.py:13
  333.2 3.0 copy-start.2
  336.2 17.6 %collective-permute-start.9 = (f32[512,128]{1,0:T(8,128)S(1)}, f32[512,128]{1,0:T(8,128)S(1)}, u32[]{:S(2)}, u32[]{:S(2)}) collective-permute-start(f32[512,128]{1,0:T(8,128)S(1)} %bitcast.125), channel_id=1, source_target_pairs={{1,0},{2,1},{3,2},{4,3},{5,4},{6,5},{7,6},{8,7},{9,8},{10,9},{11,1... | collective-permute-start | bytes 786440 | tf_op jit(solution)/shard_map/ppermute | solution.py:13
  337.5 25.6 %collective-permute-start.15 = (f32[512,128]{1,0:T(8,128)}, f32[512,128]{1,0:T(8,128)S(1)}, u32[]{:S(2)}, u32[]{:S(2)}) collective-permute-start(f32[512,128]{1,0:T(8,128)} %collective-permute-done.14), channel_id=1, source_target_pairs={{0,1},{1,2},{2,3},{3,4},{4,5},{5,6},{6,7},{7,8},{8,9},{9,10},{10,1... | collective-permute-start | bytes 786440 | tf_op jit(solution)/shard_map/ppermute | solution.py:13
  343.6 19.5 %collective-permute-start.12 = (f32[512,128]{1,0:T(8,128)}, f32[512,128]{1,0:T(8,128)S(1)}, u32[]{:S(2)}, u32[]{:S(2)}) collective-permute-start(f32[512,128]{1,0:T(8,128)} %collective-permute-done.11), channel_id=1, source_target_pairs={{1,0},{2,1},{3,2},{4,3},{5,4},{6,5},{7,6},{8,7},{9,8},{10,9},{11,1... | collective-permute-start | bytes 786440 | tf_op jit(solution)/shard_map/ppermute | solution.py:13
  344.9 23.9 %collective-permute-start.8 = (f32[512,128]{1,0:T(8,128)S(1)}, f32[512,128]{1,0:T(8,128)S(1)}, u32[]{:S(2)}, u32[]{:S(2)}) collective-permute-start(f32[512,128]{1,0:T(8,128)S(1)} %collective-permute-done.7), channel_id=1, source_target_pairs={{0,1},{1,2},{2,3},{3,4},{4,5},{5,6},{6,7},{7,8},{8,9},{9,10},{10,1... | collective-permute-start | bytes 786440 | tf_op jit(solution)/shard_map/ppermute | solution.py:13
  351.0 17.8 %collective-permute-start.5 = (f32[512,128]{1,0:T(8,128)S(1)}, f32[512,128]{1,0:T(8,128)S(1)}, u32[]{:S(2)}, u32[]{:S(2)}) collective-permute-start(f32[512,128]{1,0:T(8,128)S(1)} %collective-permute-done.4), channel_id=1, source_target_pairs={{1,0},{2,1},{3,2},{4,3},{5,4},{6,5},{7,6},{8,7},{9,8},{10,9},{11,1... | collective-permute-start | bytes 786440 | tf_op jit(solution)/shard_map/ppermute | solution.py:13
Sparse Core Ops, SparseCore 0:
  336.3 271.4 all-reduce.1
where the time goes:
time: 621 us; the launch traced here: 618 us
  waiting for transfers between devices  261 us (42%)
  other arithmetic  152 us (24%)
  local copies, waits for them, and re-layouts  81.9 us (13%)
  starting transfers between devices  49.9 us (8%)
  matrix products  49.6 us (8%)
  between operations  15 us (2%)
  loops' own time  7.98 us (1%)
    psum x1, waiting for transfers between devices, local(): weight_grad = lax.psum(scaled_part, ('dp', 'sx', 'sy'))  236 us
    scatter-add x6, other arithmetic, grad_group(): accum.at[picks.reshape(-1)]  137 us
    ppermute x12, starting transfers between devices, shifted(): return lax.ppermute(block, axis, route)  39.9 us
    transpose x6, local copies, waits for them, and re-layouts, grad_group(): jnp.einsum('gvd,kcd->kgvc', grad_rows, weights, preferred_element_type=jn...  20.1 us
    dot_general x6, matrix products, forward_group(): jnp.einsum('kgvc,kcd->gvd', gathered, weights, preferred_element_type=jnp...  18.2 us
    dot_general x6, matrix products, forward_group(): jnp.einsum('kgvc,gvd->kcd', gathered, grad_rows, preferred_element_type=j...  17.3 us
    gather x6, local copies, waits for them, and re-layouts, forward_group(): gathered = extended[picks]  16.4 us
    ppermute x12, waiting for transfers between devices, shifted(): return lax.ppermute(block, axis, route)  15 us
  transfers between devices with their start and end apart: 17, of which 4 were waited for; matrix products, arithmetic and copies ran while one was open for 44% of the time, Pallas kernels for 0%

commit v1 on v0

--- a/solution.py
+++ b/solution.py
@@ -106,7 +106,7 @@
         num_blocks * width_block * lax.axis_size("dp") * lax.axis_size("sx") * lax.axis_size("sy")
     )
     scaled_part = weight_part * (1.0 / math.sqrt(total))
-    weight_grad = lax.psum(scaled_part, ("dp", "sx", "sy"))
+    weight_grad = lax.psum(lax.psum(scaled_part, "dp"), ("sx", "sy"))
     return (output, input_grad, weight_grad)
 
 

time: 621 us -> 548 us (0.88)
  waiting for transfers between devices: 261 us -> 194 us
    psum x1 -> x2, waiting for transfers between devices: 236 us -> 161 us  [local(): weight_grad = lax.psum(lax.psum(scaled_part, 'dp'), ('sx', 'sy'))]
    ppermute x2, waiting for transfers between devices: 0.01 us -> 16.5 us  [padded(): lax.ppermute(tail, axis, [(i, (i + 1) % count) for i in range(ends)])]
    ppermute x2, waiting for transfers between devices: 9.99 us -> 0.08 us  [padded(): lax.ppermute(head, axis, [((i + 1) % count, i) for i in range(ends)])]
  transfers between devices with their start and end apart: 17 -> 18, of which waited for: 4 -> 6; matrix products, arithmetic and copies ran while one was open for 44% -> 35% of each run, Pallas kernels for 0% -> 0%
where the time goes in v1:
time: 548 us; the launch traced here: 545 us
  waiting for transfers between devices  194 us (35%)
  other arithmetic  151 us (28%)
  local copies, waits for them, and re-layouts  81.1 us (15%)
  starting transfers between devices  47.6 us (9%)
  matrix products  47.5 us (9%)
  between operations  15 us (3%)
  loops' own time  7.94 us (1%)
    psum x2, waiting for transfers between devices, local(): weight_grad = lax.psum(lax.psum(scaled_part, 'dp'), ('sx', 'sy'))  161 us
    scatter-add x6, other arithmetic, grad_group(): accum.at[picks.reshape(-1)]  138 us
    ppermute x12, starting transfers between devices, shifted(): return lax.ppermute(block, axis, route)  38.3 us
    transpose x6, local copies, waits for them, and re-layouts, grad_group(): jnp.einsum('gvd,kcd->kgvc', grad_rows, weights, preferred_element_type=jn...  20.1 us
    dot_general x6, matrix products, forward_group(): jnp.einsum('kgvc,kcd->gvd', gathered, weights, preferred_element_type=jnp...  18.2 us
    dot_general x6, matrix products, forward_group(): jnp.einsum('kgvc,gvd->kcd', gathered, grad_rows, preferred_element_type=j...  17.4 us
    ppermute x2, waiting for transfers between devices, padded(): lax.ppermute(tail, axis, [(i, (i + 1) % count) for i in range(ends)])  16.5 us
    gather x6, local copies, waits for them, and re-layouts, forward_group(): gathered = extended[picks]  16.4 us
  transfers between devices with their start and end apart: 18, of which 6 were waited for; matrix products, arithmetic and copies ran while one was open for 35% of the time, Pallas kernels for 0%

profile of v1, /device:TPU:2, one launch (start us, length us, event | category | flops | bytes accessed | tf_op | source)
XLA Modules:
  0.0 544.7 jit_solution(15785435587363703669)
XLA Ops:
  8.5 3.2 constant_dynamic-update-slice_fusion.9
  16.8 4.4 collective-permute-done
  21.2 3.7 collective-permute-start.2
  26.9 12.1 %collective-permute-done.2 = bf16[3,1,512,128]{3,2,1,0:T(8,128)(2,1)S(1)} collective-permute-done((bf16[3,1,512,128]{3,2,1,0:T(8,128)(2,1)S(1)}, bf16[3,1,512,128]{3,2,1,0:T(8,128)(2,1)S(1)}, u32[]{:S(2)}, u32[]{:S(2)}) %collective-permute-start.2) | collective-permute-done | bytes 393248 | tf_op jit(solution)/shard_map/ppermute | solution.py:24
  45.5 80.3 %while.24 = (s32[]{:T(128)}, f32[27,128,128]{2,1,0:T(8,128)}, bf16[6,4,128,128]{3,2,1,0:T(8,128)(2,1)}, s32[6]{0:T(128)}, s32[27,24]{1,0:T(8,128)}, /*index=5*/b...) while((s32[]{:T(128)}, f32[27,128,128]{2,1,0:T(8,128)}, ...), condition=%wide.region_1.0_spmd.clone, body=%wide.region_0.1_spmd.clone.sunk | while | flops 906986816 | bytes 33004880 | solution.py:101
  51.8 3.0 fusion.39
  65.2 3.0 fusion.39
  78.6 3.0 fusion.39
  91.9 3.0 fusion.39
  105.3 3.0 fusion.39
  118.7 3.0 fusion.39
  131.3 182.6 %while.23 = (s32[]{:T(128)}, f32[57,128,128]{2,1,0:T(8,128)}, s32[6]{0:T(128)S(1)}, s32[27,24]{1,0:T(8,128)}, bf16[24,128,128]{2,1,0:T(8,128)(2,1)}, /*index=5*/...) while((s32[]{:T(128)}, f32[57,128,128]{2,1,0:T(8,128)}, s32[6]{0:T(128)S(1)}, ...), condition=%wide.region_4.5_spmd, body=%wide.region_2.0_spmd.sunk | while | flops 454754624 | bytes 43486336 | solution.py:61
  135.4 3.3 copy.22
  138.8 23.0 %scatter_fusion = f32[57,128,128]{2,1,0:T(8,128)} fusion(f32[57,128,128]{2,1,0:T(8,128)} %get-tuple-element.307, s32[108]{0:T(128)S(1)} %fusion.33, f32[108,128,128]{2,1,0:T(8,128)} %bitcast.107), kind=kCustom, calls=%fused_computation.2.clone.1 | custom fusion | flops 1769472 | bytes 21234096 | tf_op jit(solution)/shard_map/while/body/eval_jaxpr/scatter-add | solution.py:55
  165.9 3.3 copy.22
  169.3 23.1 %scatter_fusion = f32[57,128,128]{2,1,0:T(8,128)} fusion(f32[57,128,128]{2,1,0:T(8,128)} %get-tuple-element.307, s32[108]{0:T(128)S(1)} %fusion.33, f32[108,128,128]{2,1,0:T(8,128)} %bitcast.107), kind=kCustom, calls=%fused_computation.2.clone.1 | custom fusion | flops 1769472 | bytes 21234096 | tf_op jit(solution)/shard_map/while/body/eval_jaxpr/scatter-add | solution.py:55
  196.5 3.3 copy.22
  199.8 22.8 %scatter_fusion = f32[57,128,128]{2,1,0:T(8,128)} fusion(f32[57,128,128]{2,1,0:T(8,128)} %get-tuple-element.307, s32[108]{0:T(128)S(1)} %fusion.33, f32[108,128,128]{2,1,0:T(8,128)} %bitcast.107), kind=kCustom, calls=%fused_computation.2.clone.1 | custom fusion | flops 1769472 | bytes 21234096 | tf_op jit(solution)/shard_map/while/body/eval_jaxpr/scatter-add | solution.py:55
  226.8 3.3 copy.22
  230.1 23.0 %scatter_fusion = f32[57,128,128]{2,1,0:T(8,128)} fusion(f32[57,128,128]{2,1,0:T(8,128)} %get-tuple-element.307, s32[108]{0:T(128)S(1)} %fusion.33, f32[108,128,128]{2,1,0:T(8,128)} %bitcast.107), kind=kCustom, calls=%fused_computation.2.clone.1 | custom fusion | flops 1769472 | bytes 21234096 | tf_op jit(solution)/shard_map/while/body/eval_jaxpr/scatter-add | solution.py:55
  257.3 3.3 copy.22
  260.6 22.9 %scatter_fusion = f32[57,128,128]{2,1,0:T(8,128)} fusion(f32[57,128,128]{2,1,0:T(8,128)} %get-tuple-element.307, s32[108]{0:T(128)S(1)} %fusion.33, f32[108,128,128]{2,1,0:T(8,128)} %bitcast.107), kind=kCustom, calls=%fused_computation.2.clone.1 | custom fusion | flops 1769472 | bytes 21234096 | tf_op jit(solution)/shard_map/while/body/eval_jaxpr/scatter-add | solution.py:55
  287.6 3.3 copy.22
  291.0 22.9 %scatter_fusion = f32[57,128,128]{2,1,0:T(8,128)} fusion(f32[57,128,128]{2,1,0:T(8,128)} %get-tuple-element.307, s32[108]{0:T(128)S(1)} %fusion.33, f32[108,128,128]{2,1,0:T(8,128)} %bitcast.107), kind=kCustom, calls=%fused_computation.2.clone.1 | custom fusion | flops 1769472 | bytes 21234096 | tf_op jit(solution)/shard_map/while/body/eval_jaxpr/scatter-add | solution.py:55
  317.5 3.6 collective-permute-start.6
  325.0 6.2 %collective-permute-start.10 = (f32[512,128]{1,0:T(8,128)S(1)}, f32[512,128]{1,0:T(8,128)S(1)}, u32[]{:S(2)}, u32[]{:S(2)}) collective-permute-start(f32[512,128]{1,0:T(8,128)S(1)} %bitcast.128), channel_id=1, source_target_pairs={{0,1},{1,2},{2,3},{3,4},{4,5},{5,6},{6,7},{7,8},{8,9},{9,10},{10,1... | collective-permute-start | bytes 786440 | tf_op jit(solution)/shard_map/ppermute | solution.py:13
  331.2 4.0 collective-permute-start.7
  339.3 6.1 %collective-permute-start.15 = (f32[512,128]{1,0:T(8,128)S(1)}, f32[512,128]{1,0:T(8,128)S(1)}, u32[]{:S(2)}, u32[]{:S(2)}) collective-permute-start(f32[512,128]{1,0:T(8,128)S(1)} %collective-permute-done.14), channel_id=1, source_target_pairs={{0,1},{1,2},{2,3},{3,4},{4,5},{5,6},{6,7},{7,8},{8,9},{9,10},{10,1... | collective-permute-start | bytes 786440 | tf_op jit(solution)/shard_map/ppermute | solution.py:13
  346.7 6.1 %collective-permute-start.8 = (f32[512,128]{1,0:T(8,128)S(1)}, f32[512,128]{1,0:T(8,128)S(1)}, u32[]{:S(2)}, u32[]{:S(2)}) collective-permute-start(f32[512,128]{1,0:T(8,128)S(1)} %collective-permute-done.7), channel_id=1, source_target_pairs={{0,1},{1,2},{2,3},{3,4},{4,5},{5,6},{6,7},{7,8},{8,9},{9,10},{10,1... | collective-permute-start | bytes 786440 | tf_op jit(solution)/shard_map/ppermute | solution.py:13
  355.6 10.1 %collective-permute-done.15 = f32[512,128]{1,0:T(8,128)S(1)} collective-permute-done((f32[512,128]{1,0:T(8,128)S(1)}, f32[512,128]{1,0:T(8,128)S(1)}, u32[]{:S(2)}, u32[]{:S(2)}) %collective-permute-start.15) | collective-permute-done | bytes 262176 | tf_op jit(solution)/shard_map/ppermute | solution.py:13
  365.7 6.0 %collective-permute-done.8 = f32[512,128]{1,0:T(8,128)S(1)} collective-permute-done((f32[512,128]{1,0:T(8,128)S(1)}, f32[512,128]{1,0:T(8,128)S(1)}, u32[]{:S(2)}, u32[]{:S(2)}) %collective-permute-start.8) | collective-permute-done | bytes 262176 | tf_op jit(solution)/shard_map/ppermute | solution.py:13
  373.6 161.4 %all-reduce.5.cloned.1.call-done = f32[27,128,128]{2,1,0:T(8,128)} async-done(((f32[27,128,128]{2,1,0:T(8,128)}), f32[27,128,128]{2,1,0:T(8,128)}) %all-reduce.5.cloned.1.call-update) | async-done | bytes 1769488 | tf_op jit(solution)/shard_map/psum | solution.py:109
  (157 shorter events, 118.9 us)
Async XLA Ops:
  7.2 330.8 %all-reduce.3.cloned.1.call-start = ((), (), s32[]{:S(2)}) async-start(), calls=%async_computation | async-start | bytes 3538944 | tf_op jit(solution)/shard_map/psum | solution.py:109
  8.5 16.4 %copy-start.3 = (s32[1,1,1,27,24]{3,4,2,1,0:T(8,128)S(1)}, s32[1,1,1,27,24]{3,4,2,1,0:T(8,128)}, u32[]{:S(2)}) copy-start(s32[1,1,1,27,24]{3,4,2,1,0:T(8,128)} %param.13) | copy-start | bytes 7780
  12.3 4.4 collective-permute-start.1
  14.3 6.9 %collective-permute-start = (bf16[1,1,512,128]{3,2,1,0:T(8,128)(2,1)S(1)}, bf16[1,1,512,128]{3,2,1,0:T(8,128)(2,1)S(1)}, u32[]{:S(2)}, u32[]{:S(2)}) collective-permute-start(bf16[1,1,512,128]{3,2,1,0:T(8,128)(2,1)S(1)} %bitcast.120), channel_id=1, source_target_pairs={{0,16},{16,32},{32,48},{1,17},{17,33},{33,49},{2,18},{18,34},{34,5... | collective-permute-start | bytes 393224 | tf_op jit(solution)/shard_map/ppermute | solution.py:24
  21.2 17.8 %collective-permute-start.2 = (bf16[3,1,512,128]{3,2,1,0:T(8,128)(2,1)S(1)}, bf16[3,1,512,128]{3,2,1,0:T(8,128)(2,1)S(1)}, u32[]{:S(2)}, u32[]{:S(2)}) collective-permute-start(bf16[3,1,512,128]{3,2,1,0:T(8,128)(2,1)S(1)} %pad_maximum_fusion), channel_id=1, source_target_pairs={{0,1},{1,2},{2,3},{3,4},{4,5},{5,6},{6,7},{7,8},{8,9},{9,10},{10,1... | collective-permute-start | bytes 1179656 | tf_op jit(solution)/shard_map/ppermute | solution.py:24
  25.6 14.7 %collective-permute-start.3 = (bf16[3,1,512,128]{3,2,1,0:T(8,128)(2,1)S(1)}, bf16[3,1,512,128]{3,2,1,0:T(8,128)(2,1)S(1)}, u32[]{:S(2)}, u32[]{:S(2)}) collective-permute-start(bf16[3,1,512,128]{3,2,1,0:T(8,128)(2,1)S(1)} %pad_maximum_fusion), channel_id=1, source_target_pairs={{1,0},{2,1},{3,2},{4,3},{5,4},{6,5},{7,6},{8,7},{9,8},{10,9},{11,1... | collective-permute-start | bytes 1179656 | tf_op jit(solution)/shard_map/ppermute | solution.py:26
  51.8 3.1 copy-start
  57.7 1.2 copy-start.1
  65.2 3.1 copy-start
  71.1 1.2 copy-start.1
  78.5 3.1 copy-start
  84.5 1.2 copy-start.1
  91.9 3.1 copy-start
  97.9 1.2 copy-start.1
  105.3 3.1 copy-start
  111.3 1.2 copy-start.1
  118.7 3.1 copy-start
  124.7 1.2 copy-start.1
  128.8 406.1 %all-reduce.5.cloned.1.call-start = ((), (), s32[]{:S(2)}) async-start(), calls=%async_computation.1 | async-start | bytes 3538944 | tf_op jit(solution)/shard_map/psum | solution.py:109
  128.9 2.4 copy-start.2
  315.6 15.6 %collective-permute-start.14 = (f32[512,128]{1,0:T(8,128)S(1)}, f32[512,128]{1,0:T(8,128)S(1)}, u32[]{:S(2)}, u32[]{:S(2)}) collective-permute-start(f32[512,128]{1,0:T(8,128)S(1)} %bitcast.132), channel_id=1, source_target_pairs={{0,16},{16,32},{32,48},{1,17},{17,33},{33,49},{2,18},{18,34},{34,5... | collective-permute-start | bytes 786440 | tf_op jit(solution)/shard_map/ppermute | solution.py:13
  317.5 17.7 %collective-permute-start.6 = (f32[512,128]{1,0:T(8,128)S(1)}, f32[512,128]{1,0:T(8,128)S(1)}, u32[]{:S(2)}, u32[]{:S(2)}) collective-permute-start(f32[512,128]{1,0:T(8,128)S(1)} %bitcast.131), channel_id=1, source_target_pairs={{16,0},{32,16},{48,32},{17,1},{33,17},{49,33},{18,2},{34,18},{50,3... | collective-permute-start | bytes 786440 | tf_op jit(solution)/shard_map/ppermute | solution.py:13
  321.1 16.8 %collective-permute-start.13 = (f32[512,128]{1,0:T(8,128)S(1)}, f32[512,128]{1,0:T(8,128)S(1)}, u32[]{:S(2)}, u32[]{:S(2)}) collective-permute-start(f32[512,128]{1,0:T(8,128)S(1)} %bitcast.130), channel_id=1, source_target_pairs={{0,16},{16,32},{32,48},{1,17},{17,33},{33,49},{2,18},{18,34},{34,5... | collective-permute-start | bytes 786440 | tf_op jit(solution)/shard_map/ppermute | solution.py:13
  323.1 16.2 %collective-permute-start.11 = (f32[512,128]{1,0:T(8,128)S(1)}, f32[512,128]{1,0:T(8,128)S(1)}, u32[]{:S(2)}, u32[]{:S(2)}) collective-permute-start(f32[512,128]{1,0:T(8,128)S(1)} %bitcast.129), channel_id=1, source_target_pairs={{0,16},{16,32},{32,48},{1,17},{17,33},{33,49},{2,18},{18,34},{34,5... | collective-permute-start | bytes 786440 | tf_op jit(solution)/shard_map/ppermute | solution.py:13
  325.0 20.3 %collective-permute-start.10 = (f32[512,128]{1,0:T(8,128)S(1)}, f32[512,128]{1,0:T(8,128)S(1)}, u32[]{:S(2)}, u32[]{:S(2)}) collective-permute-start(f32[512,128]{1,0:T(8,128)S(1)} %bitcast.128), channel_id=1, source_target_pairs={{0,1},{1,2},{2,3},{3,4},{4,5},{5,6},{6,7},{7,8},{8,9},{9,10},{10,1... | collective-permute-start | bytes 786440 | tf_op jit(solution)/shard_map/ppermute | solution.py:13
  331.2 15.5 %collective-permute-start.7 = (f32[512,128]{1,0:T(8,128)S(1)}, f32[512,128]{1,0:T(8,128)S(1)}, u32[]{:S(2)}, u32[]{:S(2)}) collective-permute-start(f32[512,128]{1,0:T(8,128)S(1)} %bitcast.127), channel_id=1, source_target_pairs={{16,0},{32,16},{48,32},{17,1},{33,17},{49,33},{18,2},{34,18},{50,3... | collective-permute-start | bytes 786440 | tf_op jit(solution)/shard_map/ppermute | solution.py:13
  335.2 17.6 %collective-permute-start.4 = (f32[512,128]{1,0:T(8,128)S(1)}, f32[512,128]{1,0:T(8,128)}, u32[]{:S(2)}, u32[]{:S(2)}) collective-permute-start(f32[512,128]{1,0:T(8,128)S(1)} %bitcast.126), channel_id=1, source_target_pairs={{16,0},{32,16},{48,32},{17,1},{33,17},{49,33},{18,2},{34,18},{50,3... | collective-permute-start | bytes 786440 | tf_op jit(solution)/shard_map/ppermute | solution.py:13
  338.0 17.6 %collective-permute-start.9 = (f32[512,128]{1,0:T(8,128)S(1)}, f32[512,128]{1,0:T(8,128)S(1)}, u32[]{:S(2)}, u32[]{:S(2)}) collective-permute-start(f32[512,128]{1,0:T(8,128)S(1)} %bitcast.125), channel_id=1, source_target_pairs={{1,0},{2,1},{3,2},{4,3},{5,4},{6,5},{7,6},{8,7},{9,8},{10,9},{11,1... | collective-permute-start | bytes 786440 | tf_op jit(solution)/shard_map/ppermute | solution.py:13
  339.3 26.4 %collective-permute-start.15 = (f32[512,128]{1,0:T(8,128)S(1)}, f32[512,128]{1,0:T(8,128)S(1)}, u32[]{:S(2)}, u32[]{:S(2)}) collective-permute-start(f32[512,128]{1,0:T(8,128)S(1)} %collective-permute-done.14), channel_id=1, source_target_pairs={{0,1},{1,2},{2,3},{3,4},{4,5},{5,6},{6,7},{7,8},{8,9},{9,10},{10,1... | collective-permute-start | bytes 786440 | tf_op jit(solution)/shard_map/ppermute | solution.py:13
  345.4 20.3 %collective-permute-start.12 = (f32[512,128]{1,0:T(8,128)S(1)}, f32[512,128]{1,0:T(8,128)S(1)}, u32[]{:S(2)}, u32[]{:S(2)}) collective-permute-start(f32[512,128]{1,0:T(8,128)S(1)} %collective-permute-done.11), channel_id=1, source_target_pairs={{1,0},{2,1},{3,2},{4,3},{5,4},{6,5},{7,6},{8,7},{9,8},{10,9},{11,1... | collective-permute-start | bytes 786440 | tf_op jit(solution)/shard_map/ppermute | solution.py:13
  346.7 25.0 %collective-permute-start.8 = (f32[512,128]{1,0:T(8,128)S(1)}, f32[512,128]{1,0:T(8,128)S(1)}, u32[]{:S(2)}, u32[]{:S(2)}) collective-permute-start(f32[512,128]{1,0:T(8,128)S(1)} %collective-permute-done.7), channel_id=1, source_target_pairs={{0,1},{1,2},{2,3},{3,4},{4,5},{5,6},{6,7},{7,8},{8,9},{9,10},{10,1... | collective-permute-start | bytes 786440 | tf_op jit(solution)/shard_map/ppermute | solution.py:13
  352.8 18.9 %collective-permute-start.5 = (f32[512,128]{1,0:T(8,128)}, f32[512,128]{1,0:T(8,128)S(1)}, u32[]{:S(2)}, u32[]{:S(2)}) collective-permute-start(f32[512,128]{1,0:T(8,128)} %collective-permute-done.4), channel_id=1, source_target_pairs={{1,0},{2,1},{3,2},{4,3},{5,4},{6,5},{7,6},{8,7},{9,8},{10,9},{11,1... | collective-permute-start | bytes 786440 | tf_op jit(solution)/shard_map/ppermute | solution.py:13
Sparse Core Ops, SparseCore 0:
  128.9 63.3 all-reduce.2
  338.1 196.8 all-reduce.4
